TPU v7x, 128 devices: a whole 4x4x4 slice. The times are simulated.
128 devices in a mesh: subj: 8 (over x, y_lo), slab: 16 (over y_hi, z, core).
Axes of the slice: x: 4, y: 4 (y_hi: 2, y_lo: 2; y = y_hi * 2 + y_lo), z: 4, core: 2. Of those that a mesh axis runs over, the one named last changes fastest.
Arguments:
- subjects: float32 [16, 128, 448, 128], P('subj', 'slab'), may hold values from -8 to 8
- templates: float32 [4, 128, 448, 128], P(None, 'slab', 'subj'), may hold values from -6 to 6
- labels: int32 [16], replicated, may hold values from 0 to 3, as said below
- group_live_counts: int32 [8], replicated, may hold values from 1 to 2, as said below
Outputs:
- new_templates: float32 [4, 128, 448, 128], P(None, 'slab', 'subj')
Inputs may be any that keep to these rules, and one draw needn't show every extreme that they name: `labels`: slot j belongs to group j // 2; slot 0 of group g has label g mod 4. The live slots of group g are its first group_live_counts[g] slots; the other slots hold volumes of no subject; some group has all 2 slots live.
All inputs are finite; a program needn't handle non-finite values.
Results may differ from a plain program's by a relative error of at most 0.00002.
Values sent between devices are 32-bit elements; how exact they have to be, the bound alone decides.
No kernel may reach another device: no remote copies, remote signals or barrier semaphores. Data moves between devices by JAX's collectives and lax.ppermute only.
A program may use at most 192 MiB of HBM per device.

v0:
```python
import jax
import jax.numpy as jnp
from jax import lax
from jax.sharding import PartitionSpec as P

RADIUS = 4


epsilon = 1e-05
step_size = 0.5


def extended(block, sides, width):
    for axis, dim in sides:
        count = lax.axis_size(axis)
        forward = [(i, i + 1) for i in range(count - 1)]
        backward = [(target, source) for source, target in forward]
        low = lax.ppermute(
            lax.slice_in_dim(block, block.shape[dim] - width, None, axis=dim), axis, forward
        )
        high = lax.ppermute(lax.slice_in_dim(block, 0, width, axis=dim), axis, backward)
        block = jnp.concatenate([low, block, high], axis=dim)
    return block


def window_sum(volume, which_axis, extent):
    running = lax.slice_in_dim(volume, 0, extent, axis=which_axis)
    for offset in range(1, 2 * RADIUS + 1):
        running = running + lax.slice_in_dim(volume, offset, offset + extent, axis=which_axis)
    return running


def padded_sum(volume, which_axis):
    widths = [(0, 0)] * volume.ndim
    widths[which_axis] = (RADIUS, RADIUS)
    return window_sum(jnp.pad(volume, widths), which_axis, volume.shape[which_axis])


def plane_box(volume, leading):
    return padded_sum(padded_sum(volume, leading), leading + 1)


def similarity_gradient(subject_ext, template_ext, slab_depth, rim):
    window = float((2 * RADIUS + 1) ** 3)
    row_count = subject_ext.shape[0] - 2 * RADIUS
    channels = jnp.stack(
        [
            subject_ext,
            template_ext,
            subject_ext * subject_ext,
            template_ext * template_ext,
            subject_ext * template_ext,
        ]
    )
    local_sums = plane_box(window_sum(channels, 1, row_count), 2)
    subject_sum = local_sums[0]
    template_sum = local_sums[1]
    covariance = local_sums[4] - subject_sum * template_sum / window
    subject_variance = local_sums[2] - subject_sum * subject_sum / window
    template_variance = local_sums[3] - template_sum * template_sum / window
    denominator = subject_variance * template_variance + epsilon
    cross_weight = 2.0 * covariance / denominator
    spread_weight = -covariance * covariance * subject_variance / (denominator * denominator)
    mean_weight = -(cross_weight * subject_sum + 2.0 * spread_weight * template_sum) / window
    stacked = jnp.stack([mean_weight, cross_weight, spread_weight])
    stacked = extended(stacked, (("slab", 1),), RADIUS)
    filtered = plane_box(window_sum(stacked, 1, slab_depth), 2)
    centre_subject = subject_ext[rim : rim + slab_depth]
    centre_template = template_ext[rim : rim + slab_depth]
    return filtered[0] + filtered[1] * centre_subject + 2.0 * filtered[2] * centre_template


def per_device(subjects, templates, labels, group_live_counts):
    rim = RADIUS
    group_index = lax.axis_index("subj")
    slot_total = subjects.shape[0]
    slab_depth = subjects.shape[1]
    clusters = templates.shape[0]
    group_total = group_live_counts.shape[0]
    slot_positions = jnp.arange(labels.shape[0], dtype=jnp.int32)
    group_ids = jnp.arange(group_total, dtype=jnp.int32)
    slot_live_counts = jnp.sum(
        jnp.where(
            (slot_positions // slot_total)[:, None] == group_ids[None, :],
            group_live_counts[None, :],
            0,
        ),
        axis=1,
    )
    live_mask = (slot_positions % slot_total < slot_live_counts).astype(jnp.float32)
    cluster_membership = (labels[:, None] == jnp.arange(clusters, dtype=jnp.int32)[None, :]).astype(
        jnp.float32
    ) * live_mask[:, None]
    members = jnp.sum(cluster_membership, axis=0)
    planes = lax.all_gather(templates, "subj", axis=2, tiled=True)
    template_ext = extended(planes, (("slab", 1),), rim)
    subject_ext = extended(subjects, (("slab", 1),), rim)
    own_labels = lax.dynamic_slice_in_dim(labels, group_index * slot_total, slot_total)
    own_load = jnp.sum(jnp.where(group_ids == group_index, group_live_counts, 0))

    def accumulate(slot_number, cluster_totals):
        cluster_label = own_labels[slot_number]
        live_weight = (slot_number < own_load).astype(jnp.float32)
        subject = lax.dynamic_index_in_dim(subject_ext, slot_number, 0, keepdims=False)
        template = lax.dynamic_index_in_dim(template_ext, cluster_label, 0, keepdims=False)
        template_gradient = similarity_gradient(subject, template, slab_depth, rim)
        current = lax.dynamic_index_in_dim(cluster_totals, cluster_label, 0, keepdims=False)
        return lax.dynamic_update_index_in_dim(
            cluster_totals, current + live_weight * template_gradient, cluster_label, 0
        )

    empty = jnp.zeros((clusters, slab_depth, subjects.shape[2], subjects.shape[3]), jnp.float32)
    cluster_totals = lax.fori_loop(0, slot_total, accumulate, empty)
    summed = lax.psum_scatter(cluster_totals, "subj", scatter_dimension=2, tiled=True)
    return templates + step_size * summed / members[:, None, None, None]


def solution(mesh):
    in_specs = (P("subj", "slab", None, None), P(None, "slab", "subj", None), P(), P())
    out_specs = P(None, "slab", "subj", None)
    return jax.shard_map(
        per_device, mesh=mesh, in_specs=in_specs, out_specs=out_specs, check_vma=False
    )
```

profile of v0, /device:TPU:103, one launch (start us, length us, event | category | flops | bytes accessed | tf_op | source)
XLA Modules:
  0.0 852.7 jit_solution(321791496275400842)
XLA Ops:
  7.3 151.5 %all-gather.2.cloned.1.call-done = f32[4,8,448,128]{3,2,1,0:T(8,128)} async-done(((f32[4,8,56,128]{3,2,1,0:T(8,128)}), f32[4,8,448,128]{3,2,1,0:T(8,128)}) %all-gather.2.cloned.1.call-update) | async-done | bytes 7340048 | tf_op jit(solution)/shard_map/all_gather | solution.py:95
  158.8 7.0 fusion.33
  165.9 8.1 collective-permute-start.4
  178.2 7.2 collective-permute-start.2
  188.1 45.7 %collective-permute-done.2 = f32[2,4,448,128]{3,2,1,0:T(8,128)S(1)} collective-permute-done((f32[2,4,448,128]{3,2,1,0:T(8,128)}, f32[2,4,448,128]{3,2,1,0:T(8,128)S(1)}, u32[]{:S(2)}, u32[]{:S(2)}) %collective-permute-start.2) | collective-permute-done | bytes 1835040 | tf_op jit(solution)/shard_map/ppermute | solution.py:18
  233.8 8.0 collective-permute-done.3
  241.8 5.1 pad_maximum_fusion.3
  246.9 8.7 %pad_maximum_fusion.2 = f32[4,16,448,128]{3,2,1,0:T(8,128)} fusion(f32[4,4,448,128]{3,2,1,0:T(8,128)} %collective-permute-done.5, f32[4,8,448,128]{3,2,1,0:T(8,128)S(1)} %bitcast.4, f32[4,4,448,128]{3,2,1,0:T(8,128)} %collective-permute-done.4), kind=kLoop, calls=%fused_computation.86 | loop fusion | flops 7340032 | bytes 29360128 | tf_op jit(solution)/shard_map/concatenate | solution.py:22
  259.4 436.6 %while.15 = (s32[]{:T(128)}, f32[4,8,448,128]{3,2,1,0:T(8,128)}, s32[2]{0:T(128)S(1)}, s32[]{:T(128)}, f32[2,16,448,128]{3,2,1,0:T(8,128)}, /*index=5*/f32[4,16,...) while((s32[]{:T(128)}, f32[4,8,448,128]{3,2,1,0:T(8,128)}, s32[2]{0:T(128)S(1)}, s32[]{:T(128)}, ...), condition=%wide.region_2.3_spmd, body=%wide.region_1.2_spmd.sunk | while | flops 122945536 | bytes 389022016 | solution.py:113
  278.3 4.4 multiply_dynamic-update-slice_fusion.8
  282.7 27.5 %slice_add_fusion.21 = f32[5,8,448,128]{3,2,1,0:T(8,128)S(1)} fusion(f32[5,16,448,128]{3,2,1,0:T(8,128)} %multiply_dynamic-update-slice_fusion.8), kind=kLoop, calls=%fused_computation.24.clone.1 | loop fusion | flops 18350080 | bytes 91750400 | tf_op jit(solution)/shard_map/while/body/eval_jaxpr/add | solution.py:29
  310.1 8.6 %slice_add_fusion.22 = f32[5,8,448,128]{3,2,1,0:T(8,128)} fusion(f32[5,8,448,128]{3,2,1,0:T(8,128)S(1)} %slice_add_fusion.21), kind=kLoop, calls=%fused_computation.32.clone.1 | loop fusion | flops 18350080 | bytes 18350080 | tf_op jit(solution)/shard_map/while/body/eval_jaxpr/add | solution.py:29
  318.8 33.1 %fusion.39 = f32[5,8,448,128]{3,2,1,0:T(8,128)S(1)} fusion(f32[5,8,448,128]{3,2,1,0:T(8,128)} %slice_add_fusion.22), kind=kLoop, calls=%fused_computation.23.clone.1 | loop fusion | flops 18350080 | bytes 18350080 | tf_op jit(solution)/shard_map/while/body/eval_jaxpr/add | solution.py:29
  363.2 27.3 %collective-permute-done = f32[3,4,448,128]{3,2,1,0:T(8,128)} collective-permute-done((f32[3,4,448,128]{3,2,1,0:T(8,128)}, f32[3,4,448,128]{3,2,1,0:T(8,128)}, u32[]{:S(2)}, u32[]{:S(2)}) %collective-permute-start) | collective-permute-done | bytes 2752544 | tf_op jit(solution)/shard_map/while/body/eval_jaxpr/ppermute | solution.py:18
  390.5 8.0 collective-permute-done.1
  398.5 9.3 %maximum_maximum_fusion.2 = (f32[3,12,448,128]{3,2,1,0:T(8,128)}, f32[3,12,448,128]{3,2,1,0:T(8,128)}) fusion(f32[1,8,448,128]{3,2,1,0:T(8,128)} %copy-done.1, f32[1,8,448,128]{3,2,1,0:T(8,128)} %copy-done, f32[1,8,448,128]{3,2,1,0:T(8,128)S(1)} %get-tuple-element.229, f32[3,4,448,128]{3,2,1,0:T(8,128)} %collective-permute-done, ...), kind=kLoop, calls=%fused_computation.38.clone.1 | loop fusion | flops 12386304 | bytes 27525120 | tf_op jit(solution)/shard_map/while/body/eval_jaxpr/concatenate | solution.py:22
  407.8 19.3 %slice_add_fusion.23 = f32[3,8,448,128]{3,2,1,0:T(8,128)} fusion(f32[3,12,448,128]{3,2,1,0:T(8,128)} %get-tuple-element.232, f32[3,12,448,128]{3,2,1,0:T(8,128)} %get-tuple-element.233, f32[1,8,448,128]{3,2,1,0:T(8,128)} %copy-done.1, f32[1,8,448,128]{3,2,1,0:T(8,128)} %copy-done, f32[1,8,448,128]{3,2,1,0:T(8,128)S(1)} %get-tuple-element.229), kind=kLoop, calls=%fused_computation.48.clone.1 | loop fusion | flops 13762560 | bytes 55050240 | tf_op jit(solution)/shard_map/while/body/eval_jaxpr/add | solution.py:29
  427.0 20.5 %slice_add_fusion.24 = f32[3,8,448,128]{3,2,1,0:T(8,128)} fusion(f32[3,8,448,128]{3,2,1,0:T(8,128)} %slice_add_fusion.23), kind=kLoop, calls=%fused_computation.57.clone.1 | loop fusion | flops 11010048 | bytes 11010048 | tf_op jit(solution)/shard_map/while/body/eval_jaxpr/add | solution.py:29
  447.5 24.2 %fusion.41 = f32[3,8,448,128]{3,2,1,0:T(8,128)} fusion(f32[3,8,448,128]{3,2,1,0:T(8,128)} %slice_add_fusion.24), kind=kLoop, calls=%fused_computation.47.clone.1 | loop fusion | flops 11010048 | bytes 11010048 | tf_op jit(solution)/shard_map/while/body/eval_jaxpr/add | solution.py:29
  471.7 6.1 fusion.42
  496.5 4.4 multiply_dynamic-update-slice_fusion.8
  501.0 27.5 %slice_add_fusion.21 = f32[5,8,448,128]{3,2,1,0:T(8,128)S(1)} fusion(f32[5,16,448,128]{3,2,1,0:T(8,128)} %multiply_dynamic-update-slice_fusion.8), kind=kLoop, calls=%fused_computation.24.clone.1 | loop fusion | flops 18350080 | bytes 91750400 | tf_op jit(solution)/shard_map/while/body/eval_jaxpr/add | solution.py:29
  528.4 8.6 %slice_add_fusion.22 = f32[5,8,448,128]{3,2,1,0:T(8,128)} fusion(f32[5,8,448,128]{3,2,1,0:T(8,128)S(1)} %slice_add_fusion.21), kind=kLoop, calls=%fused_computation.32.clone.1 | loop fusion | flops 18350080 | bytes 18350080 | tf_op jit(solution)/shard_map/while/body/eval_jaxpr/add | solution.py:29
  537.1 33.1 %fusion.39 = f32[5,8,448,128]{3,2,1,0:T(8,128)S(1)} fusion(f32[5,8,448,128]{3,2,1,0:T(8,128)} %slice_add_fusion.22), kind=kLoop, calls=%fused_computation.23.clone.1 | loop fusion | flops 18350080 | bytes 18350080 | tf_op jit(solution)/shard_map/while/body/eval_jaxpr/add | solution.py:29
  581.4 27.3 %collective-permute-done = f32[3,4,448,128]{3,2,1,0:T(8,128)} collective-permute-done((f32[3,4,448,128]{3,2,1,0:T(8,128)}, f32[3,4,448,128]{3,2,1,0:T(8,128)}, u32[]{:S(2)}, u32[]{:S(2)}) %collective-permute-start) | collective-permute-done | bytes 2752544 | tf_op jit(solution)/shard_map/while/body/eval_jaxpr/ppermute | solution.py:18
  608.7 8.0 collective-permute-done.1
  616.8 9.3 %maximum_maximum_fusion.2 = (f32[3,12,448,128]{3,2,1,0:T(8,128)}, f32[3,12,448,128]{3,2,1,0:T(8,128)}) fusion(f32[1,8,448,128]{3,2,1,0:T(8,128)} %copy-done.1, f32[1,8,448,128]{3,2,1,0:T(8,128)} %copy-done, f32[1,8,448,128]{3,2,1,0:T(8,128)S(1)} %get-tuple-element.229, f32[3,4,448,128]{3,2,1,0:T(8,128)} %collective-permute-done, ...), kind=kLoop, calls=%fused_computation.38.clone.1 | loop fusion | flops 12386304 | bytes 27525120 | tf_op jit(solution)/shard_map/while/body/eval_jaxpr/concatenate | solution.py:22
  626.0 19.3 %slice_add_fusion.23 = f32[3,8,448,128]{3,2,1,0:T(8,128)} fusion(f32[3,12,448,128]{3,2,1,0:T(8,128)} %get-tuple-element.232, f32[3,12,448,128]{3,2,1,0:T(8,128)} %get-tuple-element.233, f32[1,8,448,128]{3,2,1,0:T(8,128)} %copy-done.1, f32[1,8,448,128]{3,2,1,0:T(8,128)} %copy-done, f32[1,8,448,128]{3,2,1,0:T(8,128)S(1)} %get-tuple-element.229), kind=kLoop, calls=%fused_computation.48.clone.1 | loop fusion | flops 13762560 | bytes 55050240 | tf_op jit(solution)/shard_map/while/body/eval_jaxpr/add | solution.py:29
  645.3 20.5 %slice_add_fusion.24 = f32[3,8,448,128]{3,2,1,0:T(8,128)} fusion(f32[3,8,448,128]{3,2,1,0:T(8,128)} %slice_add_fusion.23), kind=kLoop, calls=%fused_computation.57.clone.1 | loop fusion | flops 11010048 | bytes 11010048 | tf_op jit(solution)/shard_map/while/body/eval_jaxpr/add | solution.py:29
  665.8 24.2 %fusion.41 = f32[3,8,448,128]{3,2,1,0:T(8,128)} fusion(f32[3,8,448,128]{3,2,1,0:T(8,128)} %slice_add_fusion.24), kind=kLoop, calls=%fused_computation.47.clone.1 | loop fusion | flops 11010048 | bytes 11010048 | tf_op jit(solution)/shard_map/while/body/eval_jaxpr/add | solution.py:29
  690.0 6.1 fusion.42
  696.9 146.7 %reduce-scatter.2.cloned.1.call-done = f32[4,8,56,128]{3,2,1,0:T(8,128)} async-done(((f32[4,8,448,128]{3,2,1,0:T(8,128)}), f32[4,8,56,128]{3,2,1,0:T(8,128)}) %reduce-scatter.2.cloned.1.call-update) | async-done | bytes 917520 | tf_op jit(solution)/shard_map/reduce_scatter | solution.py:114
  (66 shorter events, 69.5 us)
Async XLA Ops:
  6.5 152.3 %all-gather.2.cloned.1.call-start = ((), (), s32[]{:S(2)}) async-start(), calls=%async_computation.1 | async-start | bytes 8257536 | tf_op jit(solution)/shard_map/all_gather | solution.py:95
  7.3 836.3 %reduce-scatter.2.cloned.1.call-start = ((), (), s32[]{:S(2)}) async-start(), calls=%async_computation.2 | async-start | bytes 8257536 | tf_op jit(solution)/shard_map/reduce_scatter | solution.py:114
  158.8 17.1 %copy-start.3 = (f32[2,8,448,128]{3,2,1,0:T(8,128)S(1)}, f32[2,8,448,128]{3,2,1,0:T(8,128)}, u32[]{:S(2)}) copy-start(f32[2,8,448,128]{3,2,1,0:T(8,128)} %param.6) | copy-start | bytes 11010052
  165.9 21.5 %copy-start.7 = (s32[16]{0:T(128)S(1)}, s32[16]{0:T(128)}, u32[]{:S(2)}) copy-start(s32[16]{0:T(128)} %param.8) | copy-start | bytes 196
  165.9 21.6 %copy-start.5 = (s32[8]{0:T(128)S(1)}, s32[8]{0:T(128)}, u32[]{:S(2)}) copy-start(s32[8]{0:T(128)} %param.9) | copy-start | bytes 100
  165.9 81.0 %collective-permute-start.4 = (f32[4,4,448,128]{3,2,1,0:T(8,128)}, f32[4,4,448,128]{3,2,1,0:T(8,128)}, u32[]{:S(2)}, u32[]{:S(2)}) collective-permute-start(f32[4,4,448,128]{3,2,1,0:T(8,128)} %get-tuple-element.179), channel_id=1, source_target_pairs={{0,1},{1,2},{2,3},{3,4},{4,5},{5,6},{6,7},{7,8},{8,9},{9,10},{10,1... | collective-permute-start | bytes 11010056 | tf_op jit(solution)/shard_map/ppermute | solution.py:18
  174.0 72.9 %collective-permute-start.5 = (f32[4,4,448,128]{3,2,1,0:T(8,128)}, f32[4,4,448,128]{3,2,1,0:T(8,128)}, u32[]{:S(2)}, u32[]{:S(2)}) collective-permute-start(f32[4,4,448,128]{3,2,1,0:T(8,128)} %get-tuple-element.180), channel_id=1, source_target_pairs={{1,0},{2,1},{3,2},{4,3},{5,4},{6,5},{7,6},{8,7},{9,8},{10,9},{11,1... | collective-permute-start | bytes 11010056 | tf_op jit(solution)/shard_map/ppermute | solution.py:21
  178.2 55.6 %collective-permute-start.2 = (f32[2,4,448,128]{3,2,1,0:T(8,128)}, f32[2,4,448,128]{3,2,1,0:T(8,128)S(1)}, u32[]{:S(2)}, u32[]{:S(2)}) collective-permute-start(f32[2,4,448,128]{3,2,1,0:T(8,128)} %get-tuple-element.181), channel_id=1, source_target_pairs={{0,1},{1,2},{2,3},{3,4},{4,5},{5,6},{6,7},{7,8},{8,9},{9,10},{10,1... | collective-permute-start | bytes 5505032 | tf_op jit(solution)/shard_map/ppermute | solution.py:18
  185.4 56.4 %collective-permute-start.3 = (f32[2,4,448,128]{3,2,1,0:T(8,128)}, f32[2,4,448,128]{3,2,1,0:T(8,128)}, u32[]{:S(2)}, u32[]{:S(2)}) collective-permute-start(f32[2,4,448,128]{3,2,1,0:T(8,128)} %get-tuple-element.182), channel_id=1, source_target_pairs={{1,0},{2,1},{3,2},{4,3},{5,4},{6,5},{7,6},{8,7},{9,8},{10,9},{11,1... | collective-permute-start | bytes 5505032 | tf_op jit(solution)/shard_map/ppermute | solution.py:21
  187.4 59.4 %slice-start = ((s8[7340032]{0:T(1024)(128)(4,1)}), s8[4194304]{0:T(1024)(128)(4,1)S(1)}, s32[]{:S(2)}) async-start(s8[7340032]{0:T(1024)(128)(4,1)} %bitcast.3), calls=%async_computation.3 | async-start | bytes 8388608
  188.1 58.8 %slice-start.1 = ((s8[7340032]{0:T(1024)(128)(4,1)}), s8[3145728]{0:T(1024)(128)(4,1)S(1)}, s32[]{:S(2)}) async-start(s8[7340032]{0:T(1024)(128)(4,1)} %bitcast.3), calls=%async_computation.4 | async-start | bytes 6291456
  266.2 5.5 copy-start.2
  353.5 1.3 copy-start
  353.5 1.8 copy-start.1
  358.3 32.2 %collective-permute-start = (f32[3,4,448,128]{3,2,1,0:T(8,128)}, f32[3,4,448,128]{3,2,1,0:T(8,128)}, u32[]{:S(2)}, u32[]{:S(2)}) collective-permute-start(f32[3,4,448,128]{3,2,1,0:T(8,128)} %get-tuple-element.230), channel_id=1, source_target_pairs={{0,1},{1,2},{2,3},{3,4},{4,5},{5,6},{6,7},{7,8},{8,9},{9,10},{10,1... | collective-permute-start | bytes 8257544 | tf_op jit(solution)/shard_map/while/body/eval_jaxpr/ppermute | solution.py:18
  360.2 38.3 %collective-permute-start.1 = (f32[3,4,448,128]{3,2,1,0:T(8,128)}, f32[3,4,448,128]{3,2,1,0:T(8,128)}, u32[]{:S(2)}, u32[]{:S(2)}) collective-permute-start(f32[3,4,448,128]{3,2,1,0:T(8,128)} %get-tuple-element.231), channel_id=1, source_target_pairs={{1,0},{2,1},{3,2},{4,3},{5,4},{6,5},{7,6},{8,7},{9,8},{10,9},{11,1... | collective-permute-start | bytes 8257544 | tf_op jit(solution)/shard_map/while/body/eval_jaxpr/ppermute | solution.py:21
  484.4 5.5 copy-start.2
  571.8 1.3 copy-start
  571.8 1.8 copy-start.1
  576.5 32.2 %collective-permute-start = (f32[3,4,448,128]{3,2,1,0:T(8,128)}, f32[3,4,448,128]{3,2,1,0:T(8,128)}, u32[]{:S(2)}, u32[]{:S(2)}) collective-permute-start(f32[3,4,448,128]{3,2,1,0:T(8,128)} %get-tuple-element.230), channel_id=1, source_target_pairs={{0,1},{1,2},{2,3},{3,4},{4,5},{5,6},{6,7},{7,8},{8,9},{9,10},{10,1... | collective-permute-start | bytes 8257544 | tf_op jit(solution)/shard_map/while/body/eval_jaxpr/ppermute | solution.py:18
  578.5 38.3 %collective-permute-start.1 = (f32[3,4,448,128]{3,2,1,0:T(8,128)}, f32[3,4,448,128]{3,2,1,0:T(8,128)}, u32[]{:S(2)}, u32[]{:S(2)}) collective-permute-start(f32[3,4,448,128]{3,2,1,0:T(8,128)} %get-tuple-element.231), channel_id=1, source_target_pairs={{1,0},{2,1},{3,2},{4,3},{5,4},{6,5},{7,6},{8,7},{9,8},{10,9},{11,1... | collective-permute-start | bytes 8257544 | tf_op jit(solution)/shard_map/while/body/eval_jaxpr/ppermute | solution.py:21
  696.0 0.7 copy-start.6
  696.0 0.7 copy-start.8
  696.0 147.6 %copy-start.4 = (f32[4,8,56,128]{3,2,1,0:T(8,128)S(1)}, f32[4,8,56,128]{3,2,1,0:T(8,128)}, u32[]{:S(2)}) copy-start(f32[4,8,56,128]{3,2,1,0:T(8,128)} %param.7) | copy-start | bytes 2752516
Sparse Core Ops, SparseCore 0:
  9.0 149.8 all-gather.1
  696.2 147.3 reduce-scatter.1
where the time goes:
time: 855 us; the launch traced here: 853 us
  waiting for transfers between devices  423 us (49%)
  other arithmetic  340 us (40%)
  local copies, waits for them, and re-layouts  43 us (5%)
  starting transfers between devices  27.9 us (3%)
  between operations  13.5 us (2%)
    add x12, other arithmetic, window_sum(): running + lax.slice_in_dim(volume, offset, offset + extent, axis=which_axis)  266 us
    all_gather x1, waiting for transfers between devices, per_device(): planes = lax.all_gather(templates, 'subj', axis=2, tiled=True)  152 us
    reduce_scatter x1, waiting for transfers between devices, per_device(): lax.psum_scatter(cluster_totals, 'subj', scatter_dimension=2, tiled=True)  147 us
    ppermute x4, waiting for transfers between devices, extended(): lax.ppermute(lax.slice_in_dim(block, block.shape[dim] - width, None, axis...  100 us
    concatenate x4, other arithmetic, extended(): block = jnp.concatenate([low, block, high], axis=dim)  32.3 us
    ppermute x4, waiting for transfers between devices, extended(): lax.ppermute(lax.slice_in_dim(block, 0, width, axis=dim), axis, backward)  24 us
    while x16, local copies, waits for them, and re-layouts  22 us
    ppermute x4, starting transfers between devices, extended(): lax.ppermute(lax.slice_in_dim(block, block.shape[dim] - width, None, axis...  19.2 us
  transfers between devices with their start and end apart: 10, of which 8 were waited for; matrix products, arithmetic and copies ran while one was open for 1% of the time, Pallas kernels for 0%

commit v1 on v0

v1 whole, which is shorter than its diff:
```python
import functools

import jax
import jax.numpy as jnp
from jax import lax
from jax.experimental import pallas as pl
from jax.experimental.pallas import tpu as pltpu
from jax.sharding import PartitionSpec as P

RADIUS = 4
RIM = 2 * RADIUS
WINDOW = 2 * RADIUS + 1
INVERSE = 1.0 / float(WINDOW**3)
ROWS = 8
epsilon = 1e-05


def neighbours(block, axis):
    low, high = block
    count = lax.axis_size(axis)
    forward = [(i, i + 1) for i in range(count - 1)]
    backward = [(target, source) for source, target in forward]
    return lax.ppermute(high, axis, forward), lax.ppermute(low, axis, backward)


def window(planes):
    count = len(planes)
    outputs = count - WINDOW + 1
    prefix, suffix = list(planes), list(planes)
    for i in range(count):
        if i % WINDOW:
            prefix[i] = prefix[i - 1] + planes[i]
    for i in reversed(range(min(outputs - outputs % WINDOW + WINDOW, count) - 1)):
        if i % WINDOW == 0 and i + WINDOW <= count:
            suffix[i] = prefix[i + WINDOW - 1]
        elif i % WINDOW < WINDOW - 1:
            suffix[i] = suffix[i + 1] + planes[i]
    return [
        suffix[i] if i % WINDOW == 0 else suffix[i] + prefix[i + WINDOW - 1]
        for i in range(outputs)
    ]


def y_box(values, band_ref):
    high = values.astype(jnp.bfloat16)
    rest = values - high.astype(jnp.float32)
    middle = rest.astype(jnp.bfloat16)
    low = (rest - middle.astype(jnp.float32)).astype(jnp.bfloat16)
    both = jnp.concatenate([high, middle], axis=1)
    return jnp.dot(both, band_ref[...], preferred_element_type=jnp.float32) + jnp.dot(
        low, band_ref[: values.shape[1]], preferred_element_type=jnp.float32
    )


def zy_box(channels, columns, band_ref, out_ref):
    def step(i, carry):
        rows = pl.ds(pl.multiple_of(i * ROWS, ROWS), ROWS)
        for c, planes in enumerate(channels(rows)):
            sums = window(planes)
            boxed = y_box(jnp.concatenate(sums, axis=0), band_ref)
            for z in range(len(sums)):
                out_ref[c, z, rows, :] = boxed[z * ROWS : (z + 1) * ROWS]
        return carry

    lax.fori_loop(0, columns, step, 0)


def x_box(ref, c, z, count):
    total = ref[c, z, pl.ds(0, count), :]
    for d in range(1, WINDOW):
        total = total + ref[c, z, pl.ds(d, count), :]
    return total


def layers(refs, index, rows):
    depth = refs[0].shape[1]
    return [ref[index, z, rows, :] for ref in refs for z in range(depth)]


def template_kernel(before, own, after, band, mean_ref, var_ref, work):
    def channels(rows):
        planes = layers((before, own, after), 0, rows)
        return planes, [v * v for v in planes]

    zy_box(channels, own.shape[2] // ROWS, band, work)

    def step(z, carry):
        total = x_box(work, 0, z, mean_ref.shape[2])
        mean = total * INVERSE
        mean_ref[0, z] = mean
        var_ref[0, z] = x_box(work, 1, z, mean_ref.shape[2]) - total * mean
        return carry

    lax.fori_loop(0, mean_ref.shape[1], step, 0)


def slot_kernel(
    first, scalars, before, own, after, t_before, t_own, t_after, mean_t, var_t, band, *rest
):
    starts, rest = ([], rest) if first else (rest[:3], rest[3:])
    sum_a, sum_q, sum_p, work, coef, boxed = rest
    slot = pl.program_id(0)
    count = pl.num_programs(0)

    @pl.when(slot == 0)
    def _():
        if first:
            for ref in (sum_a, sum_q, sum_p):
                ref[...] = jnp.zeros_like(ref)
        else:
            for ref, start in zip((sum_a, sum_q, sum_p), starts):
                ref[...] = start[...]

    @pl.when(scalars[count + slot] != 0)
    def _():
        label = scalars[slot]
        x_low, x_high, z_low, z_high = (scalars[2 * count + i] for i in range(4))

        def channels(rows):
            s = layers((before, own, after), 0, rows)
            t = layers((t_before, t_own, t_after), label, rows)
            return s, [v * v for v in s], [v * w for v, w in zip(s, t)]

        zy_box(channels, own.shape[2] // ROWS, band, work)
        width = coef.shape[2]
        row = lax.broadcasted_iota(jnp.int32, (width, own.shape[3]), 0)

        def middle(z, carry):
            inside = (z >= z_low) & (z < z_high)
            low = jnp.where(inside, x_low, width)
            s_sum = x_box(work, 0, z, width)
            s_mean = s_sum * INVERSE
            s_var = x_box(work, 1, z, width) - s_sum * s_mean
            t_mean = mean_t[label, z]
            covariance = x_box(work, 2, z, width) - s_sum * t_mean
            weight = covariance / (s_var * var_t[label, z] + epsilon)
            weight = jnp.where((row >= low) & (row < x_high), weight, 0.0)
            spread = weight * s_var
            coef[0, z] = weight
            sum_a[label, z] += weight * (s_mean - spread * t_mean)
            sum_q[label, z] += weight * spread
            return carry

        lax.fori_loop(0, coef.shape[1], middle, 0)

        def weights(rows):
            return ([coef[0, z, rows, :] for z in range(coef.shape[1])],)

        zy_box(weights, width // ROWS, band, boxed)

        def close(z, carry):
            centre = own[0, z, RIM : own.shape[2] - RIM, :]
            sum_p[label, z] += x_box(boxed, 0, z, sum_p.shape[2]) * centre
            return carry

        lax.fori_loop(0, sum_p.shape[1], close, 0)


def close_kernel(scale, sum_a, sum_q, sum_p, t_own, band, out_ref, boxed):
    k = pl.program_id(0)

    def channels(rows):
        return [[ref[0, z, rows, :] for z in range(ref.shape[1])] for ref in (sum_a, sum_q)]

    zy_box(channels, sum_a.shape[2] // ROWS, band, boxed)

    def step(z, carry):
        t = t_own[0, z, RIM : t_own.shape[2] - RIM, :]
        width = out_ref.shape[2]
        total = sum_p[0, z] - x_box(boxed, 0, z, width) - x_box(boxed, 1, z, width) * t
        out_ref[0, z] = t + total * scale[k]
        return carry

    lax.fori_loop(0, out_ref.shape[1], step, 0)


def per_device(subjects, templates, labels, group_live_counts):
    slots, depth, length, lanes = subjects.shape
    clusters, _, extent, _ = templates.shape
    groups = group_live_counts.shape[0]
    padded = extent + 2 * RIM
    middle_depth, middle_extent = depth + RIM, extent + RIM
    group_index = lax.axis_index("subj")
    slab_index = lax.axis_index("slab")

    own_labels = labels.reshape(groups, slots)
    live = jnp.arange(slots, dtype=jnp.int32)[None, :] < group_live_counts[:, None]
    members = jnp.sum(
        (own_labels[:, :, None] == jnp.arange(clusters, dtype=jnp.int32)) & live[:, :, None],
        axis=(0, 1),
    ).astype(jnp.float32)
    bounds = jnp.stack(
        [
            jnp.where(group_index == 0, RADIUS, 0),
            jnp.where(group_index == groups - 1, middle_extent - RADIUS, middle_extent),
            jnp.where(slab_index == 0, RADIUS, 0),
            jnp.where(slab_index == lax.axis_size("slab") - 1, middle_depth - RADIUS, middle_depth),
        ]
    ).astype(jnp.int32)

    reach = jnp.abs(jnp.arange(lanes)[:, None] - jnp.arange(lanes)[None, :]) <= RADIUS
    band = jnp.concatenate([reach, reach], axis=0).astype(jnp.bfloat16)

    low, high = neighbours((templates[:, :, :RIM], templates[:, :, extent - RIM :]), "subj")
    t_own = jnp.concatenate([low, templates, high], axis=2)
    t_before, t_after = neighbours((t_own, t_own), "slab")

    wide = jnp.pad(subjects, ((0, 0), (0, 0), (RIM, RIM), (0, 0)))
    pieces = []
    for j in range(slots):
        chunks = jnp.stack([wide[j, :, g * extent : g * extent + padded] for g in range(groups)])
        own = lax.all_to_all(chunks, "subj", 0, 0, tiled=True)
        before, after = neighbours((own, own), "slab")
        pieces.append((before, own, after))

    def block(shape):
        return pl.BlockSpec((1,) + shape, lambda i, *_: (i,) + (0,) * len(shape))

    def whole(shape):
        return pl.BlockSpec(shape, lambda i, *_: (0,) * len(shape), pipeline_mode=pl.Buffered(1))

    t_block = (depth, padded, lanes)
    m_block = (middle_depth, middle_extent, lanes)
    o_block = (depth, extent, lanes)
    f32 = functools.partial(jax.ShapeDtypeStruct, dtype=jnp.float32)
    params = pltpu.CompilerParams(vmem_limit_bytes=60 * 1024 * 1024)

    def cost(count, size):
        return pl.CostEstimate(flops=count, bytes_accessed=size, transcendentals=0)

    mean_t, var_t = pl.pallas_call(
        template_kernel,
        grid=(clusters,),
        in_specs=[block(t_block)] * 3 + [whole(band.shape)],
        out_specs=[block(m_block)] * 2,
        out_shape=[f32((clusters,) + m_block)] * 2,
        scratch_shapes=[pltpu.VMEM((2, middle_depth, padded, lanes), jnp.float32)],
        compiler_params=params,
        cost_estimate=cost(1 << 28, 1 << 23),
        name="templates",
    )(t_before, t_own, t_after, band)

    sums = ()
    sum_shapes = [(clusters,) + m_block] * 2 + [(clusters,) + o_block]
    for j in range(slots):
        scalars = jnp.concatenate([own_labels[:, j], live[:, j].astype(jnp.int32), bounds])
        sums = pl.pallas_call(
            functools.partial(slot_kernel, j == 0),
            grid_spec=pltpu.PrefetchScalarGridSpec(
                num_scalar_prefetch=1,
                grid=(groups,),
                in_specs=[block(t_block)] * 3
                + [whole((clusters,) + t_block)] * 3
                + [whole((clusters,) + m_block)] * 2
                + [whole(band.shape)]
                + [whole(s.shape) for s in sums],
                out_specs=[whole(s) for s in sum_shapes],
                scratch_shapes=[
                    pltpu.VMEM((3, middle_depth, padded, lanes), jnp.float32),
                    pltpu.VMEM((1,) + m_block, jnp.float32),
                    pltpu.VMEM((1, depth, middle_extent, lanes), jnp.float32),
                ],
            ),
            out_shape=[f32(s) for s in sum_shapes],
            compiler_params=params,
            cost_estimate=cost(1 << 30, 1 << 25),
            name=f"slots_{j}",
        )(scalars, *pieces[j], t_before, t_own, t_after, mean_t, var_t, band, *sums)

    return pl.pallas_call(
        close_kernel,
        grid=(clusters,),
        in_specs=[pl.BlockSpec(memory_space=pltpu.SMEM)]
        + [block(m_block)] * 2
        + [block(o_block), block(t_block), whole(band.shape)],
        out_specs=block(o_block),
        out_shape=f32((clusters,) + o_block),
        scratch_shapes=[pltpu.VMEM((2, depth, middle_extent, lanes), jnp.float32)],
        compiler_params=params,
        cost_estimate=cost(1 << 28, 1 << 23),
        name="close",
    )(1.0 / members, *sums, t_own, band)


def solution(mesh):
    in_specs = (P("subj", "slab", None, None), P(None, "slab", "subj", None), P(), P())
    out_specs = P(None, "slab", "subj", None)
    return jax.shard_map(
        per_device, mesh=mesh, in_specs=in_specs, out_specs=out_specs, check_vma=False
    )
```

time: 855 us -> 251 us (0.29)
  waiting for transfers between devices: 423 us -> 77.8 us
  other arithmetic: 340 us -> 2.53 us
  Pallas kernels: 0 us -> 94.1 us
  blocking collectives: 0 us -> 31.9 us
  local copies, waits for them, and re-layouts: 43 us -> 11.6 us
  between operations: 13.5 us -> 0.17 us
    add x13 -> x0, other arithmetic: 269 us -> none  [the longest x12 266 us: window_sum(): running + lax.slice_in_dim(volume, offset, offset + extent, axis=which_axis)]
    all_gather x1 -> x0, waiting for transfers between devices: 152 us -> none  [per_device(): planes = lax.all_gather(templates, 'subj', axis=2, tiled=True)]
    reduce_scatter x1 -> x0, waiting for transfers between devices: 147 us -> none  [per_device(): lax.psum_scatter(cluster_totals, 'subj', scatter_dimension=2, tiled=True)]
    pallas_call x0 -> x4, Pallas kernels: none -> 94.1 us  [the longest x2 72.7 us: per_device(): pl.pallas_call(functools.partial(slot_kernel, j == 0), grid_spec=pltpu.Pr...]
    ppermute x8, waiting for transfers between devices: 124 us -> 77.8 us  [the longest x4 52.1 us: neighbours(): lax.ppermute(low, axis, backward)]
    concatenate x4 -> x0, other arithmetic: 32.3 us -> none  [extended(): block = jnp.concatenate([low, block, high], axis=dim)]
    all_to_all x0 -> x1, blocking collectives: none -> 31.9 us  [per_device(): own = lax.all_to_all(chunks, 'subj', 0, 0, tiled=True)]
    while x16 -> x0, local copies, waits for them, and re-layouts: 22 us -> none
  transfers between devices with their start and end apart: 10 -> 9, of which waited for: 8 -> 3; matrix products, arithmetic and copies ran while one was open for 1% -> 2% of each run, Pallas kernels for 0% -> 23%
where the time goes in v1:
time: 251 us; the launch traced here: 252 us
  Pallas kernels  94.1 us (37%)
  waiting for transfers between devices  77.8 us (31%)
  starting transfers between devices  34.3 us (14%)
  blocking collectives  31.9 us (13%)
  local copies, waits for them, and re-layouts  11.6 us (5%)
  other arithmetic  2.53 us (1%)
    pallas_call x2, Pallas kernels, per_device(): pl.pallas_call(functools.partial(slot_kernel, j == 0), grid_spec=pltpu.Pr...  72.7 us
    ppermute x4, waiting for transfers between devices, neighbours(): lax.ppermute(low, axis, backward)  52.1 us
    all_to_all x1, blocking collectives, per_device(): own = lax.all_to_all(chunks, 'subj', 0, 0, tiled=True)  31.9 us
    ppermute x4, waiting for transfers between devices, neighbours(): lax.ppermute(high, axis, forward)  25.6 us
    ppermute x4, starting transfers between devices, neighbours(): lax.ppermute(high, axis, forward)  17.4 us
    pallas_call x1, Pallas kernels, per_device(): pl.pallas_call(template_kernel, grid=(clusters,), in_specs=[block(t_block...  12.2 us
    ppermute x4, starting transfers between devices, neighbours(): lax.ppermute(low, axis, backward)  10.6 us
    pallas_call x1, Pallas kernels, per_device(): pl.pallas_call(close_kernel, grid=(clusters,), in_specs=[pl.BlockSpec(mem...  9.23 us
  transfers between devices with their start and end apart: 9, of which 3 were waited for; matrix products, arithmetic and copies ran while one was open for 2% of the time, Pallas kernels for 23%

profile of v1, /device:TPU:103, one launch (start us, length us, event | category | flops | bytes accessed | tf_op | source)
XLA Modules:
  0.0 252.4 jit_solution(4101906125165843378)
XLA Ops:
  0.0 1.9 fusion.2
  1.9 0.3 copy-done
  2.3 0.8 slice_dynamic-update-slice_fusion.5
  3.0 0.8 slice_dynamic-update-slice_fusion.4
  3.8 0.8 slice_dynamic-update-slice_fusion.3
  4.6 0.8 slice_dynamic-update-slice_fusion.2
  5.4 0.7 slice_dynamic-update-slice_fusion.1
  6.1 0.8 slice_dynamic-update-slice_fusion
  6.9 0.8 fusion.3
  7.6 31.9 %all_to_all.10.own = f32[8,8,72,128]{3,2,1,0:T(8,128)} all-to-all(f32[8,8,72,128]{3,2,1,0:T(8,128)S(1)} %get-tuple-element.23), channel_id=1, replica_groups=mesh['subj'=8,'slab'=16] {'subj'}, dimensions={0} | all-to-all | bytes 4718592 | tf_op jit(solution)/shard_map/all_to_all | solution.py:212
  39.6 6.2 %all-to-all-start = ((f32[8,8,72,128]{3,2,1,0:T(8,128)}), f32[8,8,72,128]{3,2,1,0:T(8,128)}, u32[]{:S(2)}, u32[]{:S(2)}) async-start(f32[8,8,72,128]{3,2,1,0:T(8,128)} %get-tuple-element.24), calls=%async_computation | async-start | bytes 4718592 | tf_op jit(solution)/shard_map/all_to_all | solution.py:212
  45.8 3.1 %collective-permute-start.2 = (f32[4,8,8,128]{3,2,1,0:T(8,128)S(1)}, f32[4,8,8,128]{3,2,1,0:T(8,128)S(1)}, u32[]{:S(2)}, u32[]{:S(2)}) collective-permute-start(f32[4,8,8,128]{3,2,1,0:T(8,128)S(1)} %get-tuple-element.40), channel_id=1, source_target_pairs={{0,16},{16,32},{32,48},{48,64},{64,80},{80,96},{96,112},{1,17},{17... | collective-permute-start | bytes 393224 | tf_op jit(solution)/shard_map/ppermute | solution.py:23
  48.9 3.1 %collective-permute-start.3 = (f32[4,8,8,128]{3,2,1,0:T(8,128)S(1)}, f32[4,8,8,128]{3,2,1,0:T(8,128)S(1)}, u32[]{:S(2)}, u32[]{:S(2)}) collective-permute-start(f32[4,8,8,128]{3,2,1,0:T(8,128)S(1)} %get-tuple-element.39), channel_id=1, source_target_pairs={{16,0},{32,16},{48,32},{64,48},{80,64},{96,80},{112,96},{17,1},{33... | collective-permute-start | bytes 393224 | tf_op jit(solution)/shard_map/ppermute | solution.py:23
  52.0 25.6 %collective-permute-done.2 = f32[4,8,8,128]{3,2,1,0:T(8,128)S(1)} collective-permute-done((f32[4,8,8,128]{3,2,1,0:T(8,128)S(1)}, f32[4,8,8,128]{3,2,1,0:T(8,128)S(1)}, u32[]{:S(2)}, u32[]{:S(2)}) %collective-permute-start.2) | collective-permute-done | bytes 131104 | tf_op jit(solution)/shard_map/ppermute | solution.py:23
  77.7 5.6 %collective-permute-start.4 = (f32[4,8,72,128]{3,2,1,0:T(8,128)S(1)}, f32[4,8,72,128]{3,2,1,0:T(8,128)S(1)}, u32[]{:S(2)}, u32[]{:S(2)}) collective-permute-start(f32[4,8,72,128]{3,2,1,0:T(8,128)S(1)} %constant_dynamic-update-slice_fusion.own.t_own), channel_id=1, source_target_pairs={{0,1},{1,2},{2,3},{3,4},{4,5},{5,6},{6,7},{7,8},{8,9},{9,10},{10,1... | collective-permute-start | bytes 3538952 | tf_op jit(solution)/shard_map/ppermute | solution.py:23
  83.3 1.9 collective-permute-start.6
  85.2 2.4 collective-permute-start.7
  87.6 6.8 %collective-permute-start = (f32[8,8,72,128]{3,2,1,0:T(8,128)}, f32[8,8,72,128]{3,2,1,0:T(8,128)}, u32[]{:S(2)}, u32[]{:S(2)}) collective-permute-start(f32[8,8,72,128]{3,2,1,0:T(8,128)} %all-to-all-done.own), channel_id=1, source_target_pairs={{0,1},{1,2},{2,3},{3,4},{4,5},{5,6},{6,7},{7,8},{8,9},{9,10},{10,1... | collective-permute-start | bytes 7077896 | tf_op jit(solution)/shard_map/ppermute | solution.py:23
  94.4 1.9 collective-permute-start.1
  96.4 3.2 %collective-permute-start.5 = (f32[4,8,72,128]{3,2,1,0:T(8,128)S(1)}, f32[4,8,72,128]{3,2,1,0:T(8,128)S(1)}, u32[]{:S(2)}, u32[]{:S(2)}) collective-permute-start(f32[4,8,72,128]{3,2,1,0:T(8,128)S(1)} %constant_dynamic-update-slice_fusion.own.t_own), channel_id=1, source_target_pairs={{1,0},{2,1},{3,2},{4,3},{5,4},{6,5},{7,6},{8,7},{9,8},{10,9},{11,1... | collective-permute-start | bytes 3538952 | tf_op jit(solution)/shard_map/ppermute | solution.py:23
  100.0 0.7 iota_compare_fusion.1
  100.7 0.5 fusion.6
  101.2 1.3 concatenate.17.scalars
  102.5 1.2 concatenate.14.scalars
  103.8 0.6 add_convert_fusion.band
  104.5 0.5 convert_divide_fusion.scale
  105.0 52.1 %collective-permute-done.5.after.t_after = f32[4,8,72,128]{3,2,1,0:T(8,128)S(1)} collective-permute-done((f32[4,8,72,128]{3,2,1,0:T(8,128)S(1)}, f32[4,8,72,128]{3,2,1,0:T(8,128)S(1)}, u32[]{:S(2)}, u32[]{:S(2)}) %collective-permute-start.5) | collective-permute-done | bytes 1179680 | tf_op jit(solution)/shard_map/ppermute | solution.py:23
  157.1 1.1 copy-done.3
  158.2 12.2 %templates.1 = (f32[4,16,64,128]{3,2,1,0:T(8,128)}, f32[4,16,64,128]{3,2,1,0:T(8,128)}) custom-call(f32[4,8,72,128]{3,2,1,0:T(8,128)} %copy-done.2, f32[4,8,72,128]{3,2,1,0:T(8,128)} %copy-done.1, f32[4,8,72,128]{3,2,1,0:T(8,128)} %copy-done.3, bf16[256,128]{1,0:T(8,128)(2,1)} %add_convert_fusion.band), custom_call_target="tpu_custom_call" | custom-call | flops 268435456 | bytes 8388608 | tf_op jit(solution)/shard_map/templates/pallas_call | solution.py:231
  170.5 46.1 %slots_0.1 = (f32[4,16,64,128]{3,2,1,0:T(8,128)}, f32[4,16,64,128]{3,2,1,0:T(8,128)}, f32[4,8,56,128]{3,2,1,0:T(8,128)}) custom-call(s32[20]{0:T(128)} %concatenate.17.scalars, f32[8,8,72,128]{3,2,1,0:T(8,128)} %collective-permute-done.6.before, f32[8,8,72,128]{3,2,1,0:T(8,128)} %all_to_all.10.own, f32[8,8,72,128]{3,2,1,0:T(8,128)} %collective-permute-done.7.after, ...), custom_call_target="tpu_custom_call" | custom-call | flops 1073741824 | bytes 33554432 | tf_op jit(solution)/shard_map/slots_0/pallas_call | solution.py:247
  216.6 26.5 %slots_1.1 = (f32[4,16,64,128]{3,2,1,0:T(8,128)}, f32[4,16,64,128]{3,2,1,0:T(8,128)}, f32[4,8,56,128]{3,2,1,0:T(8,128)}) custom-call(s32[20]{0:T(128)} %concatenate.14.scalars, f32[8,8,72,128]{3,2,1,0:T(8,128)} %collective-permute-done.before, f32[8,8,72,128]{3,2,1,0:T(8,128)} %all-to-all-done.own, f32[8,8,72,128]{3,2,1,0:T(8,128)} %collective-permute-done.1.after, ...), custom_call_target="tpu_custom_call" | custom-call | flops 1073741824 | bytes 33554432 | tf_op jit(solution)/shard_map/slots_1/pallas_call | solution.py:247
  243.2 9.2 %close.1 = f32[4,8,56,128]{3,2,1,0:T(8,128)} custom-call(f32[4]{0:T(128)} %convert_divide_fusion.scale, f32[4,16,64,128]{3,2,1,0:T(8,128)} %get-tuple-element.18.sum_a, f32[4,16,64,128]{3,2,1,0:T(8,128)} %get-tuple-element.19.sum_q, f32[4,8,56,128]{3,2,1,0:T(8,128)} %get-tuple-element.20.sum_p, f32[4,8,72,128]{3,2,1,0:T(8,128)} %copy-done.1, ...), custom_call_target="tpu_custom_call" | custom-call | flops 268435456 | bytes 8388608 | tf_op jit(solution)/shard_map/close/pallas_call | solution.py:270
  (26 shorter events, 0.7 us)
Async XLA Ops:
  0.0 2.3 copy-start
  39.6 6.3 %copy-start.4 = (f32[4,8,56,128]{3,2,1,0:T(8,128)S(1)}, f32[4,8,56,128]{3,2,1,0:T(8,128)}, u32[]{:S(2)}) copy-start(f32[4,8,56,128]{3,2,1,0:T(8,128)} %param.5) | copy-start | bytes 2752516
  39.6 48.1 %all-to-all-start = ((f32[8,8,72,128]{3,2,1,0:T(8,128)}), f32[8,8,72,128]{3,2,1,0:T(8,128)}, u32[]{:S(2)}, u32[]{:S(2)}) async-start(f32[8,8,72,128]{3,2,1,0:T(8,128)} %get-tuple-element.24), calls=%async_computation | async-start | bytes 4718592 | tf_op jit(solution)/shard_map/all_to_all | solution.py:212
  45.8 53.9 %copy-start.5 = (s32[16]{0:T(128)S(1)}, s32[16]{0:T(128)}, u32[]{:S(2)}) copy-start(s32[16]{0:T(128)} %param.6) | copy-start | bytes 196
  45.8 31.8 %collective-permute-start.2 = (f32[4,8,8,128]{3,2,1,0:T(8,128)S(1)}, f32[4,8,8,128]{3,2,1,0:T(8,128)S(1)}, u32[]{:S(2)}, u32[]{:S(2)}) collective-permute-start(f32[4,8,8,128]{3,2,1,0:T(8,128)S(1)} %get-tuple-element.40), channel_id=1, source_target_pairs={{0,16},{16,32},{32,48},{48,64},{64,80},{80,96},{96,112},{1,17},{17... | collective-permute-start | bytes 393224 | tf_op jit(solution)/shard_map/ppermute | solution.py:23
  48.9 28.7 %collective-permute-start.3 = (f32[4,8,8,128]{3,2,1,0:T(8,128)S(1)}, f32[4,8,8,128]{3,2,1,0:T(8,128)S(1)}, u32[]{:S(2)}, u32[]{:S(2)}) collective-permute-start(f32[4,8,8,128]{3,2,1,0:T(8,128)S(1)} %get-tuple-element.39), channel_id=1, source_target_pairs={{16,0},{32,16},{48,32},{64,48},{80,64},{96,80},{112,96},{17,1},{33... | collective-permute-start | bytes 393224 | tf_op jit(solution)/shard_map/ppermute | solution.py:23
  77.7 79.4 %copy-start.1 = (f32[4,8,72,128]{3,2,1,0:T(8,128)}, f32[4,8,72,128]{3,2,1,0:T(8,128)S(1)}, u32[]{:S(2)}) copy-start(f32[4,8,72,128]{3,2,1,0:T(8,128)S(1)} %constant_dynamic-update-slice_fusion.own.t_own) | copy-start | bytes 3538948
  77.7 18.7 %collective-permute-start.4 = (f32[4,8,72,128]{3,2,1,0:T(8,128)S(1)}, f32[4,8,72,128]{3,2,1,0:T(8,128)S(1)}, u32[]{:S(2)}, u32[]{:S(2)}) collective-permute-start(f32[4,8,72,128]{3,2,1,0:T(8,128)S(1)} %constant_dynamic-update-slice_fusion.own.t_own), channel_id=1, source_target_pairs={{0,1},{1,2},{2,3},{3,4},{4,5},{5,6},{6,7},{7,8},{8,9},{9,10},{10,1... | collective-permute-start | bytes 3538952 | tf_op jit(solution)/shard_map/ppermute | solution.py:23
  83.3 87.2 %collective-permute-start.6 = (f32[8,8,72,128]{3,2,1,0:T(8,128)}, f32[8,8,72,128]{3,2,1,0:T(8,128)}, u32[]{:S(2)}, u32[]{:S(2)}) collective-permute-start(f32[8,8,72,128]{3,2,1,0:T(8,128)} %all_to_all.10.own), channel_id=1, source_target_pairs={{0,1},{1,2},{2,3},{3,4},{4,5},{5,6},{6,7},{7,8},{8,9},{9,10},{10,1... | collective-permute-start | bytes 7077896 | tf_op jit(solution)/shard_map/ppermute | solution.py:23
  85.2 85.3 %collective-permute-start.7 = (f32[8,8,72,128]{3,2,1,0:T(8,128)}, f32[8,8,72,128]{3,2,1,0:T(8,128)}, u32[]{:S(2)}, u32[]{:S(2)}) collective-permute-start(f32[8,8,72,128]{3,2,1,0:T(8,128)} %all_to_all.10.own), channel_id=1, source_target_pairs={{1,0},{2,1},{3,2},{4,3},{5,4},{6,5},{7,6},{8,7},{9,8},{10,9},{11,1... | collective-permute-start | bytes 7077896 | tf_op jit(solution)/shard_map/ppermute | solution.py:23
  87.6 129.0 %collective-permute-start = (f32[8,8,72,128]{3,2,1,0:T(8,128)}, f32[8,8,72,128]{3,2,1,0:T(8,128)}, u32[]{:S(2)}, u32[]{:S(2)}) collective-permute-start(f32[8,8,72,128]{3,2,1,0:T(8,128)} %all-to-all-done.own), channel_id=1, source_target_pairs={{0,1},{1,2},{2,3},{3,4},{4,5},{5,6},{6,7},{7,8},{8,9},{9,10},{10,1... | collective-permute-start | bytes 7077896 | tf_op jit(solution)/shard_map/ppermute | solution.py:23
  94.4 122.2 %collective-permute-start.1 = (f32[8,8,72,128]{3,2,1,0:T(8,128)}, f32[8,8,72,128]{3,2,1,0:T(8,128)}, u32[]{:S(2)}, u32[]{:S(2)}) collective-permute-start(f32[8,8,72,128]{3,2,1,0:T(8,128)} %all-to-all-done.own), channel_id=1, source_target_pairs={{1,0},{2,1},{3,2},{4,3},{5,4},{6,5},{7,6},{8,7},{9,8},{10,9},{11,1... | collective-permute-start | bytes 7077896 | tf_op jit(solution)/shard_map/ppermute | solution.py:23
  96.4 60.7 %copy-start.2 = (f32[4,8,72,128]{3,2,1,0:T(8,128)}, f32[4,8,72,128]{3,2,1,0:T(8,128)S(1)}, u32[]{:S(2)}) copy-start(f32[4,8,72,128]{3,2,1,0:T(8,128)S(1)} %collective-permute-done.4.before.t_before) | copy-start | bytes 3538948
  96.4 60.7 %collective-permute-start.5 = (f32[4,8,72,128]{3,2,1,0:T(8,128)S(1)}, f32[4,8,72,128]{3,2,1,0:T(8,128)S(1)}, u32[]{:S(2)}, u32[]{:S(2)}) collective-permute-start(f32[4,8,72,128]{3,2,1,0:T(8,128)S(1)} %constant_dynamic-update-slice_fusion.own.t_own), channel_id=1, source_target_pairs={{1,0},{2,1},{3,2},{4,3},{5,4},{6,5},{7,6},{8,7},{9,8},{10,9},{11,1... | collective-permute-start | bytes 3538952 | tf_op jit(solution)/shard_map/ppermute | solution.py:23
  157.1 1.1 copy-start.3
